TPU v7x, 32 devices: a whole 2x2x4 slice. The times are simulated.
32 devices in a mesh: query: 8 (over z, y), store: 4 (over x, core).
Axes of the slice: x: 2, y: 2, z: 4, core: 2. Of those that a mesh axis runs over, the one named last changes fastest.
Arguments:
- in_rows: bfloat16 [8, 16384, 64], P('query', 'store'), may hold values from -6 to 6
- out_rows: bfloat16 [8, 16384, 128], P('query', 'store'), may hold values from -0.625 to 0.625
- row_doc: int32 [8, 16384], P('query', 'store'), may hold values from 0 to 31
- row_pos: int32 [8, 16384], P('query', 'store'), may hold values from 0 to 255
- doc_len: int32 [8, 128], P('query', 'store'), may hold values from 128 to 256
- eig_in: float32 [64], replicated, may hold values from 0.25 to 2
- eig_out: float32 [128], replicated, may hold values from 0.25 to 2
- basis_in: float32 [64, 64], replicated, may hold values from -0.75 to 0.75
- basis_out: float32 [128, 128], replicated, may hold values from -0.5 to 0.5
- train_feats: bfloat16 [8, 768, 8192], P('query', 'store'), may hold values from -0.0625 to 0.0625
Outputs:
- scores: bfloat16 [8, 128, 768], P('query', None, 'store')
Inputs may be any that keep to these rules, and one draw needn't show every extreme that they name: On each device the 4096 rows form 8 blocks of 512 rows in order; the rows of block j belong to documents of group j in the same store column, and row_doc names the document among that destination's 32.
All inputs are finite; a program needn't handle non-finite values.
Results may differ from a plain program's by a relative error of at most 0.0049.
Values may be sent and summed in bfloat16 or wider, within the bound.
A program may use at most 64 MiB of HBM per device.

v0:
```python
import math
import jax
import jax.numpy as jnp
from jax import lax
from jax.sharding import PartitionSpec as P

damping = 0.1
highest = lax.Precision.HIGHEST


def from_behind(x, axis, by):
    devices = lax.axis_size(axis)
    return lax.ppermute(x, axis, [(i, (i + by) % devices) for i in range(devices)])


def precondition(gradients, scaling, basis_in, basis_out):
    in_width = basis_in.shape[0]
    out_width = basis_out.shape[0]
    doc_count = gradients.shape[1] // in_width
    rotated = jnp.dot(basis_out.T, gradients, precision=highest)
    turned = jnp.dot(rotated.reshape(out_width * doc_count, in_width), basis_in, precision=highest)
    turned = turned.reshape(out_width, doc_count, in_width) * scaling[:, None, :]
    restored = jnp.dot(
        basis_out, turned.reshape(out_width, doc_count * in_width), precision=highest
    )
    final_map = jnp.dot(
        restored.reshape(out_width * doc_count, in_width), basis_in.T, precision=highest
    )
    final_map = final_map.reshape(out_width, doc_count, in_width)
    return (
        jnp.transpose(final_map, (1, 0, 2))
        .reshape(doc_count, out_width * in_width)
        .astype(jnp.bfloat16)
    )


def record(score_table, query_block, anchor, train_slab):
    partial_scores = lax.dot_general(
        query_block, train_slab, (((1,), (1,)), ((), ())), preferred_element_type=jnp.float32
    )
    return lax.dynamic_update_slice_in_dim(
        score_table, partial_scores.astype(jnp.bfloat16), anchor * query_block.shape[0], 0
    )


def on_device(
    in_rows, out_rows, row_doc, row_pos, doc_len, eig_in, eig_out, basis_in, basis_out, train_feats
):
    doc_count = doc_len.shape[1]
    in_width = in_rows.shape[2]
    packed_keys = row_doc * 65536 + row_pos
    inputs_side, grads_side, keys_side = (
        lax.all_to_all(in_rows, "query", split_axis=1, concat_axis=1, tiled=True),
        lax.all_to_all(out_rows, "query", split_axis=1, concat_axis=1, tiled=True),
        lax.all_to_all(packed_keys, "query", split_axis=1, concat_axis=1, tiled=True),
    )
    inputs_side = inputs_side[0]
    grads_side = grads_side[0]
    keys_side = keys_side[0]
    doc_of_row = keys_side // 65536
    pos_of_row = keys_side % 65536
    live_mask = (doc_of_row[:, None] == jnp.arange(doc_count, dtype=jnp.int32)[None, :]) & (
        pos_of_row[:, None] < doc_len[0][None, :]
    )
    weights = live_mask.astype(jnp.bfloat16)
    row_count = inputs_side.shape[0]
    row_span = math.gcd(row_count, 1024)

    def accumulate(turn_index, running):
        row_start = turn_index * row_span
        x_part = lax.dynamic_slice_in_dim(inputs_side, row_start, row_span, 0)
        g_part = lax.dynamic_slice_in_dim(grads_side, row_start, row_span, 0)
        w_part = lax.dynamic_slice_in_dim(weights, row_start, row_span, 0)
        spread = (w_part[:, :, None] * x_part[:, None, :]).reshape(row_span, doc_count * in_width)
        return running + lax.dot_general(
            g_part, spread, (((0,), (0,)), ((), ())), preferred_element_type=jnp.float32
        )

    gradients = jnp.zeros((grads_side.shape[1], doc_count * in_width), jnp.float32)
    gradients = lax.fori_loop(0, row_count // row_span, accumulate, gradients)
    scaling = 1.0 / (eig_out[:, None] * eig_in[None, :] + damping)
    query_block = precondition(gradients, scaling, basis_in, basis_out)
    train_slab = train_feats[0]
    store_count = lax.axis_size("store")
    own_index = lax.axis_index("store")
    score_table = jnp.zeros((store_count * doc_count, train_slab.shape[0]), jnp.bfloat16)

    def travel(carry, visit_index):
        moving, table_now = carry
        table_now = record(table_now, moving, (own_index - visit_index) % store_count, train_slab)
        moving = from_behind(moving, "store", 1)
        return ((moving, table_now), None)

    (moving, score_table), _ = lax.scan(
        travel, (query_block, score_table), jnp.arange(store_count - 1, dtype=jnp.int32)
    )
    score_table = record(
        score_table, moving, (own_index - (store_count - 1)) % store_count, train_slab
    )
    return score_table[None]


def solution(mesh):
    placed = (
        P("query", "store", None),
        P("query", "store", None),
        P("query", "store"),
        P("query", "store"),
        P("query", "store"),
        P(),
        P(),
        P(),
        P(),
        P("query", "store", None),
    )
    return jax.shard_map(
        on_device, mesh=mesh, in_specs=placed, out_specs=P("query", None, "store"), check_vma=False
    )
```

profile of v0, /device:TPU:0, one launch (start us, length us, event | category | flops | bytes accessed | tf_op | source)
XLA Modules:
  0.0 183.5 jit_solution(18066739965186172153)
XLA Ops:
  0.0 0.0 copy-start
  0.0 1.4 multiply_add_fusion
  1.4 7.3 %all-to-all-start.1 = ((s32[1,8,512]{2,0,1:T(1,128)}), s32[1,8,512]{2,0,1:T(1,128)S(1)}, u32[]{:S(2)}, u32[]{:S(2)}) async-start(s32[1,8,512]{2,0,1:T(1,128)} %bitcast.1), calls=%async_computation.1 | async-start | bytes 32768 | tf_op jit(solution)/shard_map/all_to_all | solution.py:55
  8.7 4.9 %copy.27 = bf16[1,4096,64]{2,0,1:T(2,128)(2,1)S(1)} copy(bf16[1,4096,64]{1,2,0:T(8,128)(2,1)} %param.14) | data formatting | bytes 1048576 | tf_op args[0]
  13.6 0.5 broadcast.96
  14.1 22.3 %reduce.1 = bf16[4096,64]{1,0:T(8,128)(2,1)S(1)} reduce(bf16[4096,1,64]{2,1,0:T(2,128)(2,1)S(1)} %bitcast.60, bf16[]{:T(256)} %broadcast.96), dimensions={1}, to_apply=%bitcast.31.reduce_sub_computation | reduce | bytes 1048578
  36.4 1.5 reshape.110
  37.9 0.0 all-to-all-done.1
  37.9 6.0 %all-to-all-start.2 = ((bf16[8,2,16384]{2,1,0:T(2,128)(2,1)}), bf16[8,2,16384]{2,1,0:T(2,128)(2,1)}, u32[]{:S(2)}, u32[]{:S(2)}) async-start(bf16[8,2,16384]{2,1,0:T(2,128)(2,1)} %reshape.110), calls=%async_computation.2 | async-start | bytes 1048576 | tf_op jit(solution)/shard_map/all_to_all | solution.py:53
  43.9 3.2 %copy.39 = bf16[1,4096,128]{2,0,1:T(2,128)(2,1)S(1)} copy(bf16[1,4096,128]{2,1,0:T(8,128)(2,1)} %param.15) | data formatting | bytes 2097152 | tf_op args[1]
  47.1 0.0 copy-start.3
  47.1 0.0 copy-start.4
  47.1 0.0 copy-start.5
  47.1 22.3 %reduce = bf16[4096,128]{1,0:T(8,128)(2,1)S(1)} reduce(bf16[4096,1,128]{2,1,0:T(2,128)(2,1)S(1)} %bitcast.62, bf16[]{:T(256)} %broadcast.96), dimensions={1}, to_apply=%bitcast.45.reduce_sub_computation | reduce | bytes 2097154
  69.5 1.1 reshape.108
  70.6 0.0 all-to-all-done.2
  70.6 6.0 %all-to-all-start = ((bf16[8,2,32768]{2,1,0:T(2,128)(2,1)}), bf16[8,2,32768]{2,1,0:T(2,128)(2,1)}, u32[]{:S(2)}, u32[]{:S(2)}) async-start(bf16[8,2,32768]{2,1,0:T(2,128)(2,1)} %reshape.108), calls=%async_computation | async-start | bytes 2097152 | tf_op jit(solution)/shard_map/all_to_all | solution.py:54
  76.6 0.1 add_divide_fusion
  76.8 0.1 fusion.6
  76.9 4.1 %reshape.111 = bf16[4096,1,64]{2,1,0:T(2,128)(2,1)S(1)} reshape(bf16[8,2,16384]{2,1,0:T(2,128)(2,1)} %all-to-all-done.2) | data formatting | bytes 1048576
  81.0 3.6 %copy.28 = bf16[1,4096,64]{1,2,0:T(8,128)(2,1)} copy(bf16[1,4096,64]{2,0,1:T(2,128)(2,1)S(1)} %bitcast.59) | data formatting | bytes 1048576 | tf_op jit(solution)/shard_map/all_to_all | solution.py:53
  84.7 16.9 %all-to-all-done = bf16[8,2,32768]{2,1,0:T(2,128)(2,1)} async-done(((bf16[8,2,32768]{2,1,0:T(2,128)(2,1)}), bf16[8,2,32768]{2,1,0:T(2,128)(2,1)}, u32[]{:S(2)}, u32[]{:S(2)}) %all-to-all-start) | async-done | bytes 1048608 | tf_op jit(solution)/shard_map/all_to_all | solution.py:54
  101.5 4.3 %reshape.109 = bf16[4096,1,128]{2,1,0:T(2,128)(2,1)S(1)} reshape(bf16[8,2,32768]{2,1,0:T(2,128)(2,1)} %all-to-all-done) | data formatting | bytes 2097152
  105.9 1.1 copy.38
  107.0 28.7 %while.29 = (s32[]{:T(128)}, f32[128,2048]{1,0:T(8,128)S(1)}, bf16[4096,128]{1,0:T(8,128)(2,1)}, bf16[4096,32]{0,1:T(8,128)(2,1)S(1)}, bf16[4096,64]{0,1:T(8,128...) while((s32[]{:T(128)}, f32[128,2048]{1,0:T(8,128)S(1)}, bf16[4096,128]{1,0:T(8,128)(2,1)}, ...), condition=%wide.region_1.2_spmd.clone, body=%wide.region_0.1_spmd.clone.sunk | while | flops 539492352 | bytes 11337897 | solution.py:80
  107.0 0.9 constant_dynamic-slice_fusion.4
  107.9 2.2 %broadcast_multiply_fusion.2 = bf16[1024,32,64]{0,2,1:T(8,128)(2,1)} fusion(bf16[1024,64]{0,1:T(8,128)(2,1)S(1)} %constant_dynamic-slice_fusion.4, bf16[1024,32]{0,1:T(8,128)(2,1)S(1)} %constant_dynamic-slice_fusion.5), kind=kLoop, calls=%fused_computation.3.clone.1 | loop fusion | flops 2097152 | bytes 4390912 | tf_op jit(solution)/shard_map/while/body/eval_jaxpr/mul | solution.py:74
  110.1 4.0 %convolution_add_fusion.2 = f32[128,2048]{1,0:T(8,128)S(1)} fusion(bf16[1024,2048]{0,1:T(8,128)(2,1)} %bitcast.56, f32[128,2048]{1,0:T(8,128)S(1)} %get-tuple-element.306, pred[]{:T(512)S(6)} %compare.16, bf16[4096,128]{1,0:T(8,128)(2,1)} %get-tuple-element.316, s32[]{:T(128)S(6)} %select_n.65), kind=kOutput, calls=%fused_computation.2.clone.1 | convolution fusion | flops 537395200 | bytes 6553605 | tf_op jit(solution)/shard_map/while/body/eval_jaxpr/dot_general | solution.py:75
  114.1 0.9 constant_dynamic-slice_fusion.4
  115.1 2.2 %broadcast_multiply_fusion.2 = bf16[1024,32,64]{0,2,1:T(8,128)(2,1)} fusion(bf16[1024,64]{0,1:T(8,128)(2,1)S(1)} %constant_dynamic-slice_fusion.4, bf16[1024,32]{0,1:T(8,128)(2,1)S(1)} %constant_dynamic-slice_fusion.5), kind=kLoop, calls=%fused_computation.3.clone.1 | loop fusion | flops 2097152 | bytes 4390912 | tf_op jit(solution)/shard_map/while/body/eval_jaxpr/mul | solution.py:74
  117.3 4.0 %convolution_add_fusion.2 = f32[128,2048]{1,0:T(8,128)S(1)} fusion(bf16[1024,2048]{0,1:T(8,128)(2,1)} %bitcast.56, f32[128,2048]{1,0:T(8,128)S(1)} %get-tuple-element.306, pred[]{:T(512)S(6)} %compare.16, bf16[4096,128]{1,0:T(8,128)(2,1)} %get-tuple-element.316, s32[]{:T(128)S(6)} %select_n.65), kind=kOutput, calls=%fused_computation.2.clone.1 | convolution fusion | flops 537395200 | bytes 6553605 | tf_op jit(solution)/shard_map/while/body/eval_jaxpr/dot_general | solution.py:75
  121.3 0.9 constant_dynamic-slice_fusion.4
  122.3 2.2 %broadcast_multiply_fusion.2 = bf16[1024,32,64]{0,2,1:T(8,128)(2,1)} fusion(bf16[1024,64]{0,1:T(8,128)(2,1)S(1)} %constant_dynamic-slice_fusion.4, bf16[1024,32]{0,1:T(8,128)(2,1)S(1)} %constant_dynamic-slice_fusion.5), kind=kLoop, calls=%fused_computation.3.clone.1 | loop fusion | flops 2097152 | bytes 4390912 | tf_op jit(solution)/shard_map/while/body/eval_jaxpr/mul | solution.py:74
  124.5 4.0 %convolution_add_fusion.2 = f32[128,2048]{1,0:T(8,128)S(1)} fusion(bf16[1024,2048]{0,1:T(8,128)(2,1)} %bitcast.56, f32[128,2048]{1,0:T(8,128)S(1)} %get-tuple-element.306, pred[]{:T(512)S(6)} %compare.16, bf16[4096,128]{1,0:T(8,128)(2,1)} %get-tuple-element.316, s32[]{:T(128)S(6)} %select_n.65), kind=kOutput, calls=%fused_computation.2.clone.1 | convolution fusion | flops 537395200 | bytes 6553605 | tf_op jit(solution)/shard_map/while/body/eval_jaxpr/dot_general | solution.py:75
  128.5 0.9 constant_dynamic-slice_fusion.4
  129.4 2.2 %broadcast_multiply_fusion.2 = bf16[1024,32,64]{0,2,1:T(8,128)(2,1)} fusion(bf16[1024,64]{0,1:T(8,128)(2,1)S(1)} %constant_dynamic-slice_fusion.4, bf16[1024,32]{0,1:T(8,128)(2,1)S(1)} %constant_dynamic-slice_fusion.5), kind=kLoop, calls=%fused_computation.3.clone.1 | loop fusion | flops 2097152 | bytes 4390912 | tf_op jit(solution)/shard_map/while/body/eval_jaxpr/mul | solution.py:74
  131.7 4.0 %convolution_add_fusion.2 = f32[128,2048]{1,0:T(8,128)S(1)} fusion(bf16[1024,2048]{0,1:T(8,128)(2,1)} %bitcast.56, f32[128,2048]{1,0:T(8,128)S(1)} %get-tuple-element.306, pred[]{:T(512)S(6)} %compare.16, bf16[4096,128]{1,0:T(8,128)(2,1)} %get-tuple-element.316, s32[]{:T(128)S(6)} %select_n.65), kind=kOutput, calls=%fused_computation.2.clone.1 | convolution fusion | flops 537395200 | bytes 6553605 | tf_op jit(solution)/shard_map/while/body/eval_jaxpr/dot_general | solution.py:75
  135.7 1.8 fusion.12
  137.5 1.1 convolution_multiply_fusion
  138.6 0.0 copy-start.1
  138.6 1.0 fusion.13
  139.6 1.9 %fusion.3 = bf16[32,128,64]{1,2,0:T(8,128)(2,1)} fusion(f32[128,32,64]{0,2,1:T(8,128)S(1)} %bitcast.66, f32[64,64]{1,0:T(8,128)S(1)} %copy-done.2), kind=kOutput, calls=%fused_computation.10 | convolution fusion | flops 201588736 | bytes 1589248 | tf_op jit(solution)/shard_map/dot_general | solution.py:26
  141.5 2.4 %copy.30 = bf16[32,128,64]{2,1,0:T(8,128)(2,1)} copy(bf16[32,128,64]{1,2,0:T(8,128)(2,1)} %fusion.3) | data formatting | bytes 1048576 | tf_op jit(solution)/shard_map/convert_element_type | solution.py:33
  143.9 2.7 %convert_element_type.24 = bf16[32,8192]{1,0:T(8,128)(2,1)} reshape(bf16[32,128,64]{2,1,0:T(8,128)(2,1)} %copy.30) | data formatting | bytes 1048576 | tf_op jit(solution)/shard_map/convert_element_type | solution.py:33
  146.6 32.4 %while.28 = (s32[]{:T(128)}, bf16[32,8192]{1,0:T(8,128)(2,1)}, bf16[128,192]{1,0:T(8,128)(2,1)S(1)}, bf16[192,8192]{1,0:T(8,128)(2,1)S(1)}, s32[3]{0:T(128)S(1)}...) while((s32[]{:T(128)}, bf16[32,8192]{1,0:T(8,128)(2,1)}, ...), condition=%wide.region_3.4_spmd, body=%wide.region_2.3_spmd.sunk | while | flops 100669456 | bytes 6832468 | solution.py:94
  146.6 1.9 %copy.51 = bf16[32,8192]{1,0:T(8,128)(2,1)} copy(bf16[32,8192]{1,0:T(8,128)(2,1)} %get-tuple-element.336) | data formatting | bytes 1048576 | tf_op jit(solution)/shard_map
  148.5 0.0 collective-permute-start
  148.5 0.6 dynamic_slice.39
  149.7 2.1 %fusion.31 = bf16[128,192]{1,0:T(8,128)(2,1)S(1)} fusion(bf16[128,192]{1,0:T(8,128)(2,1)S(1)} %get-tuple-element.337, s32[]{:T(128)S(6)} %select_n.64, bf16[32,8192]{1,0:T(8,128)(2,1)} %copy.51, bf16[192,8192]{1,0:T(8,128)(2,1)S(1)} %get-tuple-element.350), kind=kOutput, calls=%fused_computation.1.clone.1 | convolution fusion | flops 100669440 | bytes 3686404 | tf_op jit(solution)/shard_map/while/body/eval_jaxpr/dot_general | solution.py:38
  151.8 5.6 %collective-permute-done = bf16[32,8192]{1,0:T(8,128)(2,1)} collective-permute-done((bf16[32,8192]{1,0:T(8,128)(2,1)}, bf16[32,8192]{1,0:T(8,128)(2,1)}, u32[]{:S(2)}, u32[]{:S(2)}) %collective-permute-start) | collective-permute-done | bytes 524320 | tf_op jit(solution)/shard_map/while/body/eval_jaxpr/ppermute | solution.py:13
  157.4 1.9 %copy.51 = bf16[32,8192]{1,0:T(8,128)(2,1)} copy(bf16[32,8192]{1,0:T(8,128)(2,1)} %get-tuple-element.336) | data formatting | bytes 1048576 | tf_op jit(solution)/shard_map
  159.3 0.0 collective-permute-start
  159.3 0.6 dynamic_slice.39
  160.5 2.1 %fusion.31 = bf16[128,192]{1,0:T(8,128)(2,1)S(1)} fusion(bf16[128,192]{1,0:T(8,128)(2,1)S(1)} %get-tuple-element.337, s32[]{:T(128)S(6)} %select_n.64, bf16[32,8192]{1,0:T(8,128)(2,1)} %copy.51, bf16[192,8192]{1,0:T(8,128)(2,1)S(1)} %get-tuple-element.350), kind=kOutput, calls=%fused_computation.1.clone.1 | convolution fusion | flops 100669440 | bytes 3686404 | tf_op jit(solution)/shard_map/while/body/eval_jaxpr/dot_general | solution.py:38
  162.6 5.6 %collective-permute-done = bf16[32,8192]{1,0:T(8,128)(2,1)} collective-permute-done((bf16[32,8192]{1,0:T(8,128)(2,1)}, bf16[32,8192]{1,0:T(8,128)(2,1)}, u32[]{:S(2)}, u32[]{:S(2)}) %collective-permute-start) | collective-permute-done | bytes 524320 | tf_op jit(solution)/shard_map/while/body/eval_jaxpr/ppermute | solution.py:13
  168.2 1.9 %copy.51 = bf16[32,8192]{1,0:T(8,128)(2,1)} copy(bf16[32,8192]{1,0:T(8,128)(2,1)} %get-tuple-element.336) | data formatting | bytes 1048576 | tf_op jit(solution)/shard_map
  170.1 0.0 collective-permute-start
  170.1 0.6 dynamic_slice.39
  171.2 2.1 %fusion.31 = bf16[128,192]{1,0:T(8,128)(2,1)S(1)} fusion(bf16[128,192]{1,0:T(8,128)(2,1)S(1)} %get-tuple-element.337, s32[]{:T(128)S(6)} %select_n.64, bf16[32,8192]{1,0:T(8,128)(2,1)} %copy.51, bf16[192,8192]{1,0:T(8,128)(2,1)S(1)} %get-tuple-element.350), kind=kOutput, calls=%fused_computation.1.clone.1 | convolution fusion | flops 100669440 | bytes 3686404 | tf_op jit(solution)/shard_map/while/body/eval_jaxpr/dot_general | solution.py:38
  173.4 5.6 %collective-permute-done = bf16[32,8192]{1,0:T(8,128)(2,1)} collective-permute-done((bf16[32,8192]{1,0:T(8,128)(2,1)}, bf16[32,8192]{1,0:T(8,128)(2,1)}, u32[]{:S(2)}, u32[]{:S(2)}) %collective-permute-start) | collective-permute-done | bytes 524320 | tf_op jit(solution)/shard_map/while/body/eval_jaxpr/ppermute | solution.py:13
  179.0 0.7 copy.31
  179.7 2.1 %fusion.4 = bf16[1,32,192]{2,1,0:T(8,128)(2,1)S(1)} fusion(bf16[32,8192]{1,0:T(8,128)(2,1)} %get-tuple-element.180, bf16[1,192,8192]{2,1,0:T(8,128)(2,1)S(1)} %bitcast.58), kind=kOutput, calls=%fused_computation.12 | convolution fusion | flops 100669440 | bytes 3682304 | tf_op jit(solution)/shard_map/dot_general | solution.py:38
  181.8 0.1 copy.32
  181.9 1.6 dynamic_update_slice.10
  (15 shorter events, 0.1 us)
Async XLA Ops:
  0.0 135.7 %copy-start = (f32[128,128]{1,0:T(8,128)S(1)}, f32[128,128]{1,0:T(8,128)}, u32[]{:S(2)}) copy-start(f32[128,128]{1,0:T(8,128)} %param.22) | copy-start | bytes 196612
  1.4 36.5 %all-to-all-start.1 = ((s32[1,8,512]{2,0,1:T(1,128)}), s32[1,8,512]{2,0,1:T(1,128)S(1)}, u32[]{:S(2)}, u32[]{:S(2)}) async-start(s32[1,8,512]{2,0,1:T(1,128)} %bitcast.1), calls=%async_computation.1 | async-start | bytes 32768 | tf_op jit(solution)/shard_map/all_to_all | solution.py:55
  37.9 32.6 %all-to-all-start.2 = ((bf16[8,2,16384]{2,1,0:T(2,128)(2,1)}), bf16[8,2,16384]{2,1,0:T(2,128)(2,1)}, u32[]{:S(2)}, u32[]{:S(2)}) async-start(bf16[8,2,16384]{2,1,0:T(2,128)(2,1)} %reshape.110), calls=%async_computation.2 | async-start | bytes 1048576 | tf_op jit(solution)/shard_map/all_to_all | solution.py:53
  47.1 29.5 %copy-start.3 = (f32[64]{0:T(128)S(1)}, f32[64]{0:T(128)}, u32[]{:S(2)}) copy-start(f32[64]{0:T(128)} %param.19) | copy-start | bytes 772
  47.1 29.5 %copy-start.4 = (f32[128]{0:T(128)S(1)}, f32[128]{0:T(128)}, u32[]{:S(2)}) copy-start(f32[128]{0:T(128)} %param.20) | copy-start | bytes 1540
  47.1 29.6 %copy-start.5 = (s32[1,32]{1,0:T(1,128)S(1)}, s32[1,32]{1,0:T(1,128)}, u32[]{:S(2)}) copy-start(s32[1,32]{1,0:T(1,128)} %param.18) | copy-start | bytes 388
  70.6 31.0 %all-to-all-start = ((bf16[8,2,32768]{2,1,0:T(2,128)(2,1)}), bf16[8,2,32768]{2,1,0:T(2,128)(2,1)}, u32[]{:S(2)}, u32[]{:S(2)}) async-start(bf16[8,2,32768]{2,1,0:T(2,128)(2,1)} %reshape.108), calls=%async_computation | async-start | bytes 2097152 | tf_op jit(solution)/shard_map/all_to_all | solution.py:54
  107.0 30.5 %copy-start.2 = (f32[64,64]{1,0:T(8,128)S(1)}, f32[64,64]{1,0:T(8,128)}, u32[]{:S(2)}) copy-start(f32[64,64]{1,0:T(8,128)} %param.21) | copy-start | bytes 49156
  138.6 8.0 %copy-start.1 = (bf16[1,192,8192]{2,1,0:T(8,128)(2,1)S(1)}, bf16[1,192,8192]{2,1,0:T(8,128)(2,1)}, u32[]{:S(2)}) copy-start(bf16[1,192,8192]{2,1,0:T(8,128)(2,1)} %param.23) | copy-start | bytes 9437188
  148.5 8.9 %collective-permute-start = (bf16[32,8192]{1,0:T(8,128)(2,1)}, bf16[32,8192]{1,0:T(8,128)(2,1)}, u32[]{:S(2)}, u32[]{:S(2)}) collective-permute-start(bf16[32,8192]{1,0:T(8,128)(2,1)} %copy.51), channel_id=1, source_target_pairs={{0,1},{1,2},{2,3},{3,0},{4,5},{5,6},{6,7},{7,4},{8,9},{9,10},{10,1... | collective-permute-start | bytes 1572872 | tf_op jit(solution)/shard_map/while/body/eval_jaxpr/ppermute | solution.py:13
  159.3 8.9 %collective-permute-start = (bf16[32,8192]{1,0:T(8,128)(2,1)}, bf16[32,8192]{1,0:T(8,128)(2,1)}, u32[]{:S(2)}, u32[]{:S(2)}) collective-permute-start(bf16[32,8192]{1,0:T(8,128)(2,1)} %copy.51), channel_id=1, source_target_pairs={{0,1},{1,2},{2,3},{3,0},{4,5},{5,6},{6,7},{7,4},{8,9},{9,10},{10,1... | collective-permute-start | bytes 1572872 | tf_op jit(solution)/shard_map/while/body/eval_jaxpr/ppermute | solution.py:13
  170.1 8.9 %collective-permute-start = (bf16[32,8192]{1,0:T(8,128)(2,1)}, bf16[32,8192]{1,0:T(8,128)(2,1)}, u32[]{:S(2)}, u32[]{:S(2)}) collective-permute-start(bf16[32,8192]{1,0:T(8,128)(2,1)} %copy.51), channel_id=1, source_target_pairs={{0,1},{1,2},{2,3},{3,0},{4,5},{5,6},{6,7},{7,4},{8,9},{9,10},{10,1... | collective-permute-start | bytes 1572872 | tf_op jit(solution)/shard_map/while/body/eval_jaxpr/ppermute | solution.py:13
where the time goes:
time: 185 us; the launch traced here: 184 us
  other arithmetic  55.2 us (30%)
  local copies, waits for them, and re-layouts  43 us (23%)
  waiting for transfers between devices  33.7 us (18%)
  matrix products  30.1 us (16%)
  starting transfers between devices  19.3 us (10%)
  loops' own time  1.96 us (1%)
    unnamed x3, other arithmetic  44.6 us
    unnamed x20, local copies, waits for them, and re-layouts  20.8 us
    all_to_all x1, waiting for transfers between devices, on_device(): lax.all_to_all(out_rows, 'query', split_axis=1, concat_axis=1, tiled=True)  16.9 us
    ppermute x3, waiting for transfers between devices, from_behind(): lax.ppermute(x, axis, [(i, (i + by) % devices) for i in range(devices)])  16.9 us
    dot_general x4, matrix products, accumulate(): lax.dot_general(g_part, spread, (((0,), (0,)), ((), ())), preferred_eleme...  15.9 us
    mul x4, other arithmetic, accumulate(): w_part[:, :, None] * x_part[:, None, :]  8.93 us
    dot_general x4, matrix products, record(): lax.dot_general(query_block, train_slab, (((1,), (1,)), ((), ())), prefer...  8.42 us
    all_to_all x1, starting transfers between devices, on_device(): lax.all_to_all(packed_keys, 'query', split_axis=1, concat_axis=1, tiled=T...  7.31 us
  transfers between devices with their start and end apart: 6, of which 4 were waited for; matrix products, arithmetic and copies ran while one was open for 39% of the time, Pallas kernels for 0%

commit v1 on v0

--- a/solution.py
+++ b/solution.py
@@ -6,6 +6,15 @@
 
 damping = 0.1
 highest = lax.Precision.HIGHEST
+
+
+def _start_rates(xx, which_axis, on_dim, dimension_no):
+    return jnp.concatenate(
+        lax.all_to_all(
+            jnp.stack(jnp.split(xx, lax.axis_size(which_axis), axis=on_dim)), which_axis, 0, 0
+        ),
+        axis=dimension_no,
+    )
 
 
 def from_behind(x, axis, by):
@@ -50,7 +59,7 @@
     in_width = in_rows.shape[2]
     packed_keys = row_doc * 65536 + row_pos
     inputs_side, grads_side, keys_side = (
-        lax.all_to_all(in_rows, "query", split_axis=1, concat_axis=1, tiled=True),
+        _start_rates(in_rows, "query", on_dim=1, dimension_no=1),
         lax.all_to_all(out_rows, "query", split_axis=1, concat_axis=1, tiled=True),
         lax.all_to_all(packed_keys, "query", split_axis=1, concat_axis=1, tiled=True),
     )

time: 185 us -> 168 us (0.908)
  other arithmetic: 55.2 us -> 33 us
  waiting for transfers between devices: 33.7 us -> 39.1 us
    unnamed x3 -> x2, other arithmetic: 44.6 us -> 22.4 us
    all_to_all x1, waiting for transfers between devices: 16.9 us -> 22.7 us  [on_device(): lax.all_to_all(out_rows, 'query', split_axis=1, concat_axis=1, tiled=True)]
    all_to_all x1 -> x0, local copies, waits for them, and re-layouts: 3.63 us -> none  [on_device(): lax.all_to_all(in_rows, 'query', split_axis=1, concat_axis=1, tiled=True)]
    unnamed x20 -> x25, local copies, waits for them, and re-layouts: 20.8 us -> 22.4 us
    another operation x3 -> x4, local copies, waits for them, and re-layouts: 5.6 us -> 7.08 us
  transfers between devices with their start and end apart: 6 -> 6, of which waited for: 4 -> 4; matrix products, arithmetic and copies ran while one was open for 39% -> 30% of each run, Pallas kernels for 0% -> 0%
where the time goes in v1:
time: 168 us; the launch traced here: 167 us
  local copies, waits for them, and re-layouts  42.6 us (25%)
  waiting for transfers between devices  39.1 us (23%)
  other arithmetic  33 us (20%)
  matrix products  30.2 us (18%)
  starting transfers between devices  19.3 us (11%)
  loops' own time  2.26 us (1%)
    all_to_all x1, waiting for transfers between devices, on_device(): lax.all_to_all(out_rows, 'query', split_axis=1, concat_axis=1, tiled=True)  22.7 us
    unnamed x2, other arithmetic  22.4 us
    unnamed x25, local copies, waits for them, and re-layouts  22.4 us
    ppermute x3, waiting for transfers between devices, from_behind(): lax.ppermute(x, axis, [(i, (i + by) % devices) for i in range(devices)])  16.4 us
    dot_general x4, matrix products, accumulate(): lax.dot_general(g_part, spread, (((0,), (0,)), ((), ())), preferred_eleme...  16 us
    mul x4, other arithmetic, accumulate(): w_part[:, :, None] * x_part[:, None, :]  8.92 us
    dot_general x4, matrix products, record(): lax.dot_general(query_block, train_slab, (((1,), (1,)), ((), ())), prefer...  8.42 us
    all_to_all x1, starting transfers between devices, on_device(): lax.all_to_all(packed_keys, 'query', split_axis=1, concat_axis=1, tiled=T...  7.31 us
  transfers between devices with their start and end apart: 6, of which 4 were waited for; matrix products, arithmetic and copies ran while one was open for 30% of the time, Pallas kernels for 0%

profile of v1, /device:TPU:0, one launch (start us, length us, event | category | flops | bytes accessed | tf_op | source)
XLA Modules:
  0.0 166.7 jit_solution(5619117374517007296)
XLA Ops:
  0.0 1.4 multiply_add_fusion
  1.4 7.3 %all-to-all-start.1 = ((s32[1,8,512]{2,0,1:T(1,128)}), s32[1,8,512]{2,0,1:T(1,128)S(1)}, u32[]{:S(2)}, u32[]{:S(2)}) async-start(s32[1,8,512]{2,0,1:T(1,128)} %bitcast.1), calls=%async_computation.1 | async-start | bytes 32768 | tf_op jit(solution)/shard_map/all_to_all | solution.py:64
  8.7 1.5 bitcast_dynamic-update-slice_fusion.7
  10.2 1.5 bitcast_dynamic-update-slice_fusion.6
  11.6 1.5 bitcast_dynamic-update-slice_fusion.5
  13.1 1.5 bitcast_dynamic-update-slice_fusion.4
  14.6 1.5 bitcast_dynamic-update-slice_fusion.3
  16.0 1.5 bitcast_dynamic-update-slice_fusion.2
  17.5 1.5 bitcast_dynamic-update-slice_fusion.1
  18.9 1.5 bitcast_dynamic-update-slice_fusion
  20.4 0.0 all-to-all-done.1
  20.4 6.0 %all-to-all-start.2 = ((bf16[8,1,512,64]{2,3,1,0:T(8,128)(2,1)}), bf16[8,1,512,64]{2,3,1,0:T(8,128)(2,1)}, u32[]{:S(2)}, u32[]{:S(2)}) async-start(bf16[8,1,512,64]{2,3,1,0:T(8,128)(2,1)} %bitcast_dynamic-update-slice_fusion), calls=%async_computation.2 | async-start | bytes 1048576 | tf_op jit(solution)/shard_map/all_to_all | solution.py:13
  26.4 3.2 %copy.40 = bf16[1,4096,128]{2,0,1:T(2,128)(2,1)S(1)} copy(bf16[1,4096,128]{2,1,0:T(8,128)(2,1)} %param.15) | data formatting | bytes 2097152 | tf_op args[1]
  29.6 0.5 broadcast.96
  30.1 22.4 %reduce = bf16[4096,128]{1,0:T(8,128)(2,1)S(1)} reduce(bf16[4096,1,128]{2,1,0:T(2,128)(2,1)S(1)} %bitcast.79, bf16[]{:T(256)} %broadcast.96), dimensions={1}, to_apply=%bitcast.64.reduce_sub_computation | reduce | bytes 2097154
  52.5 1.1 reshape.108
  53.7 0.0 all-to-all-done.2
  53.7 6.0 %all-to-all-start = ((bf16[8,2,32768]{2,1,0:T(2,128)(2,1)}), bf16[8,2,32768]{2,1,0:T(2,128)(2,1)}, u32[]{:S(2)}, u32[]{:S(2)}) async-start(bf16[8,2,32768]{2,1,0:T(2,128)(2,1)} %reshape.108), calls=%async_computation | async-start | bytes 2097152 | tf_op jit(solution)/shard_map/all_to_all | solution.py:63
  59.7 0.1 add_divide_fusion
  59.8 0.1 fusion.6
  60.0 1.9 %copy.35 = bf16[8,8,8,512]{3,1,2,0:T(8,128)(2,1)} copy(bf16[8,8,8,512]{3,1,0,2:T(8,128)(2,1)} %bitcast.49) | data formatting | bytes 1048576
  61.9 22.7 %all-to-all-done = bf16[8,2,32768]{2,1,0:T(2,128)(2,1)} async-done(((bf16[8,2,32768]{2,1,0:T(2,128)(2,1)}), bf16[8,2,32768]{2,1,0:T(2,128)(2,1)}, u32[]{:S(2)}, u32[]{:S(2)}) %all-to-all-start) | async-done | bytes 1048608 | tf_op jit(solution)/shard_map/all_to_all | solution.py:63
  84.6 4.3 %reshape.109 = bf16[4096,1,128]{2,1,0:T(2,128)(2,1)S(1)} reshape(bf16[8,2,32768]{2,1,0:T(2,128)(2,1)} %all-to-all-done) | data formatting | bytes 2097152
  88.9 1.1 copy.39
  90.0 28.8 %while.29 = (s32[]{:T(128)}, f32[128,2048]{1,0:T(8,128)S(1)}, bf16[4096,128]{1,0:T(8,128)(2,1)}, bf16[4096,32]{0,1:T(8,128)(2,1)S(1)}, bf16[4096,64]{0,1:T(8,128...) while((s32[]{:T(128)}, f32[128,2048]{1,0:T(8,128)S(1)}, bf16[4096,128]{1,0:T(8,128)(2,1)}, ...), condition=%wide.region_1.2_spmd.clone, body=%wide.region_0.1_spmd.clone.sunk | while | flops 539492352 | bytes 11337897 | solution.py:89
  90.0 0.9 constant_dynamic-slice_fusion.4
  91.0 2.2 %broadcast_multiply_fusion.2 = bf16[1024,32,64]{0,2,1:T(8,128)(2,1)} fusion(bf16[1024,64]{0,1:T(8,128)(2,1)S(1)} %constant_dynamic-slice_fusion.4, bf16[1024,32]{0,1:T(8,128)(2,1)S(1)} %constant_dynamic-slice_fusion.5), kind=kLoop, calls=%fused_computation.3.clone.1 | loop fusion | flops 2097152 | bytes 4390912 | tf_op jit(solution)/shard_map/while/body/eval_jaxpr/mul | solution.py:83
  93.2 4.0 %convolution_add_fusion.2 = f32[128,2048]{1,0:T(8,128)S(1)} fusion(bf16[1024,2048]{0,1:T(8,128)(2,1)} %bitcast.75, f32[128,2048]{1,0:T(8,128)S(1)} %get-tuple-element.301, pred[]{:T(512)S(6)} %compare.16, bf16[4096,128]{1,0:T(8,128)(2,1)} %get-tuple-element.311, s32[]{:T(128)S(6)} %select_n.65), kind=kOutput, calls=%fused_computation.2.clone.1 | convolution fusion | flops 537395200 | bytes 6553605 | tf_op jit(solution)/shard_map/while/body/eval_jaxpr/dot_general | solution.py:84
  97.2 0.9 constant_dynamic-slice_fusion.4
  98.2 2.2 %broadcast_multiply_fusion.2 = bf16[1024,32,64]{0,2,1:T(8,128)(2,1)} fusion(bf16[1024,64]{0,1:T(8,128)(2,1)S(1)} %constant_dynamic-slice_fusion.4, bf16[1024,32]{0,1:T(8,128)(2,1)S(1)} %constant_dynamic-slice_fusion.5), kind=kLoop, calls=%fused_computation.3.clone.1 | loop fusion | flops 2097152 | bytes 4390912 | tf_op jit(solution)/shard_map/while/body/eval_jaxpr/mul | solution.py:83
  100.4 4.0 %convolution_add_fusion.2 = f32[128,2048]{1,0:T(8,128)S(1)} fusion(bf16[1024,2048]{0,1:T(8,128)(2,1)} %bitcast.75, f32[128,2048]{1,0:T(8,128)S(1)} %get-tuple-element.301, pred[]{:T(512)S(6)} %compare.16, bf16[4096,128]{1,0:T(8,128)(2,1)} %get-tuple-element.311, s32[]{:T(128)S(6)} %select_n.65), kind=kOutput, calls=%fused_computation.2.clone.1 | convolution fusion | flops 537395200 | bytes 6553605 | tf_op jit(solution)/shard_map/while/body/eval_jaxpr/dot_general | solution.py:84
  104.4 0.9 constant_dynamic-slice_fusion.4
  105.4 2.2 %broadcast_multiply_fusion.2 = bf16[1024,32,64]{0,2,1:T(8,128)(2,1)} fusion(bf16[1024,64]{0,1:T(8,128)(2,1)S(1)} %constant_dynamic-slice_fusion.4, bf16[1024,32]{0,1:T(8,128)(2,1)S(1)} %constant_dynamic-slice_fusion.5), kind=kLoop, calls=%fused_computation.3.clone.1 | loop fusion | flops 2097152 | bytes 4390912 | tf_op jit(solution)/shard_map/while/body/eval_jaxpr/mul | solution.py:83
  107.6 4.0 %convolution_add_fusion.2 = f32[128,2048]{1,0:T(8,128)S(1)} fusion(bf16[1024,2048]{0,1:T(8,128)(2,1)} %bitcast.75, f32[128,2048]{1,0:T(8,128)S(1)} %get-tuple-element.301, pred[]{:T(512)S(6)} %compare.16, bf16[4096,128]{1,0:T(8,128)(2,1)} %get-tuple-element.311, s32[]{:T(128)S(6)} %select_n.65), kind=kOutput, calls=%fused_computation.2.clone.1 | convolution fusion | flops 537395200 | bytes 6553605 | tf_op jit(solution)/shard_map/while/body/eval_jaxpr/dot_general | solution.py:84
  111.6 0.9 constant_dynamic-slice_fusion.4
  112.6 2.2 %broadcast_multiply_fusion.2 = bf16[1024,32,64]{0,2,1:T(8,128)(2,1)} fusion(bf16[1024,64]{0,1:T(8,128)(2,1)S(1)} %constant_dynamic-slice_fusion.4, bf16[1024,32]{0,1:T(8,128)(2,1)S(1)} %constant_dynamic-slice_fusion.5), kind=kLoop, calls=%fused_computation.3.clone.1 | loop fusion | flops 2097152 | bytes 4390912 | tf_op jit(solution)/shard_map/while/body/eval_jaxpr/mul | solution.py:83
  114.8 4.0 %convolution_add_fusion.2 = f32[128,2048]{1,0:T(8,128)S(1)} fusion(bf16[1024,2048]{0,1:T(8,128)(2,1)} %bitcast.75, f32[128,2048]{1,0:T(8,128)S(1)} %get-tuple-element.301, pred[]{:T(512)S(6)} %compare.16, bf16[4096,128]{1,0:T(8,128)(2,1)} %get-tuple-element.311, s32[]{:T(128)S(6)} %select_n.65), kind=kOutput, calls=%fused_computation.2.clone.1 | convolution fusion | flops 537395200 | bytes 6553605 | tf_op jit(solution)/shard_map/while/body/eval_jaxpr/dot_general | solution.py:84
  118.8 1.8 %fusion.12 = f32[2048,128]{1,0:T(8,128)S(1)} fusion(f32[128,2048]{1,0:T(8,128)S(1)} %get-tuple-element.178, f32[128,128]{1,0:T(8,128)S(1)} %copy-done), kind=kOutput, calls=%fused_computation.39 | convolution fusion | flops 402653184 | bytes 2162688 | tf_op jit(solution)/shard_map/dot_general | solution.py:29
  120.7 1.0 convolution_multiply_fusion
  121.7 0.0 copy-start.1
  121.7 1.0 fusion.13
  122.7 1.9 %fusion.3 = bf16[32,128,64]{1,2,0:T(8,128)(2,1)} fusion(f32[128,32,64]{0,2,1:T(8,128)S(1)} %bitcast.83, f32[64,64]{1,0:T(8,128)S(1)} %copy-done.2), kind=kOutput, calls=%fused_computation.10 | convolution fusion | flops 201588736 | bytes 1589248 | tf_op jit(solution)/shard_map/dot_general | solution.py:35
  124.6 2.4 %copy.29 = bf16[32,128,64]{2,1,0:T(8,128)(2,1)} copy(bf16[32,128,64]{1,2,0:T(8,128)(2,1)} %fusion.3) | data formatting | bytes 1048576 | tf_op jit(solution)/shard_map/convert_element_type | solution.py:42
  127.0 2.7 %convert_element_type.24 = bf16[32,8192]{1,0:T(8,128)(2,1)} reshape(bf16[32,128,64]{2,1,0:T(8,128)(2,1)} %copy.29) | data formatting | bytes 1048576 | tf_op jit(solution)/shard_map/convert_element_type | solution.py:42
  129.7 32.4 %while.28 = (s32[]{:T(128)}, bf16[32,8192]{1,0:T(8,128)(2,1)}, bf16[128,192]{1,0:T(8,128)(2,1)S(1)}, bf16[192,8192]{1,0:T(8,128)(2,1)S(1)}, s32[3]{0:T(128)S(1)}...) while((s32[]{:T(128)}, bf16[32,8192]{1,0:T(8,128)(2,1)}, ...), condition=%wide.region_3.4_spmd, body=%wide.region_2.3_spmd.sunk | while | flops 100669456 | bytes 6832468 | solution.py:103
  129.7 1.9 %copy.59 = bf16[32,8192]{1,0:T(8,128)(2,1)} copy(bf16[32,8192]{1,0:T(8,128)(2,1)} %get-tuple-element.331) | data formatting | bytes 1048576 | tf_op jit(solution)/shard_map
  131.6 0.0 collective-permute-start
  131.6 0.6 dynamic_slice.39
  133.0 2.1 %fusion.31 = bf16[128,192]{1,0:T(8,128)(2,1)S(1)} fusion(bf16[128,192]{1,0:T(8,128)(2,1)S(1)} %get-tuple-element.332, s32[]{:T(128)S(6)} %select_n.64, bf16[32,8192]{1,0:T(8,128)(2,1)} %copy.59, bf16[192,8192]{1,0:T(8,128)(2,1)S(1)} %get-tuple-element.345), kind=kOutput, calls=%fused_computation.1.clone.1 | convolution fusion | flops 100669440 | bytes 3686404 | tf_op jit(solution)/shard_map/while/body/eval_jaxpr/dot_general | solution.py:47
  135.1 5.5 %collective-permute-done = bf16[32,8192]{1,0:T(8,128)(2,1)} collective-permute-done((bf16[32,8192]{1,0:T(8,128)(2,1)}, bf16[32,8192]{1,0:T(8,128)(2,1)}, u32[]{:S(2)}, u32[]{:S(2)}) %collective-permute-start) | collective-permute-done | bytes 524320 | tf_op jit(solution)/shard_map/while/body/eval_jaxpr/ppermute | solution.py:22
  140.5 1.9 %copy.59 = bf16[32,8192]{1,0:T(8,128)(2,1)} copy(bf16[32,8192]{1,0:T(8,128)(2,1)} %get-tuple-element.331) | data formatting | bytes 1048576 | tf_op jit(solution)/shard_map
  142.4 0.0 collective-permute-start
  142.4 0.6 dynamic_slice.39
  143.8 2.1 %fusion.31 = bf16[128,192]{1,0:T(8,128)(2,1)S(1)} fusion(bf16[128,192]{1,0:T(8,128)(2,1)S(1)} %get-tuple-element.332, s32[]{:T(128)S(6)} %select_n.64, bf16[32,8192]{1,0:T(8,128)(2,1)} %copy.59, bf16[192,8192]{1,0:T(8,128)(2,1)S(1)} %get-tuple-element.345), kind=kOutput, calls=%fused_computation.1.clone.1 | convolution fusion | flops 100669440 | bytes 3686404 | tf_op jit(solution)/shard_map/while/body/eval_jaxpr/dot_general | solution.py:47
  145.9 5.5 %collective-permute-done = bf16[32,8192]{1,0:T(8,128)(2,1)} collective-permute-done((bf16[32,8192]{1,0:T(8,128)(2,1)}, bf16[32,8192]{1,0:T(8,128)(2,1)}, u32[]{:S(2)}, u32[]{:S(2)}) %collective-permute-start) | collective-permute-done | bytes 524320 | tf_op jit(solution)/shard_map/while/body/eval_jaxpr/ppermute | solution.py:22
  151.3 1.9 %copy.59 = bf16[32,8192]{1,0:T(8,128)(2,1)} copy(bf16[32,8192]{1,0:T(8,128)(2,1)} %get-tuple-element.331) | data formatting | bytes 1048576 | tf_op jit(solution)/shard_map
  153.2 0.0 collective-permute-start
  153.2 0.6 dynamic_slice.39
  154.5 2.1 %fusion.31 = bf16[128,192]{1,0:T(8,128)(2,1)S(1)} fusion(bf16[128,192]{1,0:T(8,128)(2,1)S(1)} %get-tuple-element.332, s32[]{:T(128)S(6)} %select_n.64, bf16[32,8192]{1,0:T(8,128)(2,1)} %copy.59, bf16[192,8192]{1,0:T(8,128)(2,1)S(1)} %get-tuple-element.345), kind=kOutput, calls=%fused_computation.1.clone.1 | convolution fusion | flops 100669440 | bytes 3686404 | tf_op jit(solution)/shard_map/while/body/eval_jaxpr/dot_general | solution.py:47
  156.7 5.5 %collective-permute-done = bf16[32,8192]{1,0:T(8,128)(2,1)} collective-permute-done((bf16[32,8192]{1,0:T(8,128)(2,1)}, bf16[32,8192]{1,0:T(8,128)(2,1)}, u32[]{:S(2)}, u32[]{:S(2)}) %collective-permute-start) | collective-permute-done | bytes 524320 | tf_op jit(solution)/shard_map/while/body/eval_jaxpr/ppermute | solution.py:22
  162.1 0.7 copy.30
  162.8 2.1 %fusion.4 = bf16[1,32,192]{2,1,0:T(8,128)(2,1)S(1)} fusion(bf16[32,8192]{1,0:T(8,128)(2,1)} %get-tuple-element.180, bf16[1,192,8192]{2,1,0:T(8,128)(2,1)S(1)} %bitcast.77), kind=kOutput, calls=%fused_computation.12 | convolution fusion | flops 100669440 | bytes 3682304 | tf_op jit(solution)/shard_map/dot_general | solution.py:47
  164.9 0.1 copy.31
  165.1 1.6 dynamic_update_slice.10
  (19 shorter events, 0.1 us)
Async XLA Ops:
  0.0 118.8 %copy-start = (f32[128,128]{1,0:T(8,128)S(1)}, f32[128,128]{1,0:T(8,128)}, u32[]{:S(2)}) copy-start(f32[128,128]{1,0:T(8,128)} %param.22) | copy-start | bytes 196612
  1.4 19.0 %all-to-all-start.1 = ((s32[1,8,512]{2,0,1:T(1,128)}), s32[1,8,512]{2,0,1:T(1,128)S(1)}, u32[]{:S(2)}, u32[]{:S(2)}) async-start(s32[1,8,512]{2,0,1:T(1,128)} %bitcast.1), calls=%async_computation.1 | async-start | bytes 32768 | tf_op jit(solution)/shard_map/all_to_all | solution.py:64
  20.4 33.2 %all-to-all-start.2 = ((bf16[8,1,512,64]{2,3,1,0:T(8,128)(2,1)}), bf16[8,1,512,64]{2,3,1,0:T(8,128)(2,1)}, u32[]{:S(2)}, u32[]{:S(2)}) async-start(bf16[8,1,512,64]{2,3,1,0:T(8,128)(2,1)} %bitcast_dynamic-update-slice_fusion), calls=%async_computation.2 | async-start | bytes 1048576 | tf_op jit(solution)/shard_map/all_to_all | solution.py:13
  30.1 29.6 %copy-start.3 = (f32[64]{0:T(128)S(1)}, f32[64]{0:T(128)}, u32[]{:S(2)}) copy-start(f32[64]{0:T(128)} %param.19) | copy-start | bytes 772
  30.1 29.6 %copy-start.4 = (f32[128]{0:T(128)S(1)}, f32[128]{0:T(128)}, u32[]{:S(2)}) copy-start(f32[128]{0:T(128)} %param.20) | copy-start | bytes 1540
  30.1 29.7 %copy-start.5 = (s32[1,32]{1,0:T(1,128)S(1)}, s32[1,32]{1,0:T(1,128)}, u32[]{:S(2)}) copy-start(s32[1,32]{1,0:T(1,128)} %param.18) | copy-start | bytes 388
  53.7 31.0 %all-to-all-start = ((bf16[8,2,32768]{2,1,0:T(2,128)(2,1)}), bf16[8,2,32768]{2,1,0:T(2,128)(2,1)}, u32[]{:S(2)}, u32[]{:S(2)}) async-start(bf16[8,2,32768]{2,1,0:T(2,128)(2,1)} %reshape.108), calls=%async_computation | async-start | bytes 2097152 | tf_op jit(solution)/shard_map/all_to_all | solution.py:63
  90.0 30.6 %copy-start.2 = (f32[64,64]{1,0:T(8,128)S(1)}, f32[64,64]{1,0:T(8,128)}, u32[]{:S(2)}) copy-start(f32[64,64]{1,0:T(8,128)} %param.21) | copy-start | bytes 49156
  121.7 8.0 %copy-start.1 = (bf16[1,192,8192]{2,1,0:T(8,128)(2,1)S(1)}, bf16[1,192,8192]{2,1,0:T(8,128)(2,1)}, u32[]{:S(2)}) copy-start(bf16[1,192,8192]{2,1,0:T(8,128)(2,1)} %param.23) | copy-start | bytes 9437188
  131.6 8.9 %collective-permute-start = (bf16[32,8192]{1,0:T(8,128)(2,1)}, bf16[32,8192]{1,0:T(8,128)(2,1)}, u32[]{:S(2)}, u32[]{:S(2)}) collective-permute-start(bf16[32,8192]{1,0:T(8,128)(2,1)} %copy.59), channel_id=1, source_target_pairs={{0,1},{1,2},{2,3},{3,0},{4,5},{5,6},{6,7},{7,4},{8,9},{9,10},{10,1... | collective-permute-start | bytes 1572872 | tf_op jit(solution)/shard_map/while/body/eval_jaxpr/ppermute | solution.py:22
  142.4 8.9 %collective-permute-start = (bf16[32,8192]{1,0:T(8,128)(2,1)}, bf16[32,8192]{1,0:T(8,128)(2,1)}, u32[]{:S(2)}, u32[]{:S(2)}) collective-permute-start(bf16[32,8192]{1,0:T(8,128)(2,1)} %copy.59), channel_id=1, source_target_pairs={{0,1},{1,2},{2,3},{3,0},{4,5},{5,6},{6,7},{7,4},{8,9},{9,10},{10,1... | collective-permute-start | bytes 1572872 | tf_op jit(solution)/shard_map/while/body/eval_jaxpr/ppermute | solution.py:22
  153.2 8.9 %collective-permute-start = (bf16[32,8192]{1,0:T(8,128)(2,1)}, bf16[32,8192]{1,0:T(8,128)(2,1)}, u32[]{:S(2)}, u32[]{:S(2)}) collective-permute-start(bf16[32,8192]{1,0:T(8,128)(2,1)} %copy.59), channel_id=1, source_target_pairs={{0,1},{1,2},{2,3},{3,0},{4,5},{5,6},{6,7},{7,4},{8,9},{9,10},{10,1... | collective-permute-start | bytes 1572872 | tf_op jit(solution)/shard_map/while/body/eval_jaxpr/ppermute | solution.py:22
